TPU v7x, 512 devices: a whole 4x8x8 slice. The times are simulated.
512 devices in a mesh: ctx: 32 (over y_lo, z, core), exp: 16 (over x, y_hi).
Axes of the slice: x: 4, y: 8 (y_hi: 4, y_lo: 2; y = y_hi * 2 + y_lo), z: 8, core: 2. Of those that a mesh axis runs over, the one named last changes fastest.
Arguments:
- queries: bfloat16 [16, 4096, 256], P('exp', 'ctx'), may hold values from -200 to 200
- keys: bfloat16 [16, 4096, 256], P('exp', 'ctx'), may hold values from -200 to 200
- values: bfloat16 [16, 4096, 256], P('exp', 'ctx'), may hold values from -12 to 12
- experts_chosen: int32 [2, 16, 4096, 2], P(None, 'exp', 'ctx'), may hold values from 0 to 7, all different within a row; in each aligned block of 128 rows (0 to 127, 128 to 255, ..., all dimensions but the last counted through in order) at most 40 rows name the same one
- gate_scores: float32 [2, 16, 4096, 2], P(None, 'exp', 'ctx'), may hold values from 0.1 to 1
- out_weight: bfloat16 [16, 128, 4096], P('exp'), may hold values from -0.5 to 0.5
- cotangent: bfloat16 [16, 4096, 4096], P('exp', 'ctx'), may hold values from -6 to 6
Outputs:
- block_out: float32 [16, 4096, 4096], P('exp', 'ctx')
- out_weight_grad: float32 [16, 128, 4096], P('exp', None, 'ctx')
- attended_grad: float32 [16, 4096, 256], P('exp', 'ctx')
Inputs may be any that keep to these rules, and one draw needn't show every extreme that they name: `experts_chosen`: each position names two different experts of each head. Within the 128 positions of one device, for one head, no expert is named more than 40 times, a bound that some block reaches.
All inputs are finite; a program needn't handle non-finite values.
Results may differ from a plain program's by a relative error of at most 0.0065.
Values may be sent and summed in bfloat16 or wider, within the bound.
No kernel may reach another device: no remote copies, remote signals or barrier semaphores. Data moves between devices by JAX's collectives and lax.ppermute only.
A program may use at most 64 MiB of HBM per device.

v0:
```python
import jax
import jax.numpy as jnp
from jax import lax
from jax.sharding import PartitionSpec as P

EXPERTS = 8
CAP = 40


def slot_tables(chosen, gates):
    head_count = chosen.shape[0]
    tok_rows = chosen.shape[1]
    flat_ids = chosen.reshape(head_count, tok_rows * 2)
    onehot = (flat_ids[..., None] == jnp.arange(EXPERTS, dtype=jnp.int32)).astype(jnp.int32)
    slot_rank = jnp.sum((jnp.cumsum(onehot, axis=1) - 1) * onehot, axis=2)
    slot_hit = onehot[..., None] * (
        slot_rank[:, :, None, None] == jnp.arange(CAP, dtype=jnp.int32)
    ).astype(jnp.int32)
    token_of = jnp.arange(tok_rows * 2, dtype=jnp.int32) // 2
    token_table = jnp.sum(slot_hit * token_of[None, :, None, None], axis=1)
    gate_table = jnp.sum(
        slot_hit.astype(jnp.float32) * gates.reshape(head_count, tok_rows * 2)[:, :, None, None],
        axis=1,
    )
    return (flat_ids * CAP + slot_rank, token_table, gate_table)


def per_device(queries, keys, values, experts_chosen, gate_scores, out_weight, cotangent):
    tok_rows = queries.shape[1]
    head_count = experts_chosen.shape[0]
    head_size = out_weight.shape[1]
    model_width = out_weight.shape[2]
    local_experts = out_weight.shape[0]
    group_count = lax.axis_size("exp")
    first_row = lax.axis_index("ctx") * tok_rows
    score_scale = 1.0 / jnp.sqrt(jnp.float32(head_size))
    query_rows = queries[0].reshape(tok_rows, head_count, head_size)
    query_pos = first_row + jnp.arange(tok_rows, dtype=jnp.int32)
    start_state = (
        jnp.full((head_count, tok_rows), -1e30, jnp.float32),
        jnp.zeros((head_count, tok_rows), jnp.float32),
        jnp.zeros((head_count, tok_rows, head_size), jnp.float32),
    )
    key_piece = lax.all_gather(keys, "ctx", axis=1, tiled=True)
    value_piece = lax.all_gather(values, "ctx", axis=1, tiled=True)
    key_count = key_piece.shape[1]

    def compute(state_now):
        row_best, row_total, weighted_sum = state_now
        key_rows = key_piece[0].reshape(key_count, head_count, head_size)
        value_rows = value_piece[0].reshape(key_count, head_count, head_size)
        scores = (
            jnp.einsum("qhd,khd->hqk", query_rows, key_rows, preferred_element_type=jnp.float32)
            * score_scale
        )
        allowed = jnp.arange(key_count, dtype=jnp.int32)[None, :] <= query_pos[:, None]
        scores = jnp.where(allowed[None], scores, -1e30)
        new_best = jnp.maximum(row_best, jnp.max(scores, axis=-1))
        weights = jnp.where(allowed[None], jnp.exp(scores - new_best[..., None]), 0.0)
        row_total = jnp.sum(weights, axis=-1)
        update = jnp.einsum(
            "hqk,khd->hqd",
            weights.astype(jnp.bfloat16),
            value_rows,
            preferred_element_type=jnp.float32,
        )
        weighted_sum = update
        return (new_best, row_total, weighted_sum)

    row_best, row_total, weighted_sum = lax.cond(
        jnp.int32(0) > first_row + tok_rows - 1, lambda state_now: state_now, compute, start_state
    )
    attended = (weighted_sum / row_total[..., None]).transpose(1, 0, 2).astype(jnp.bfloat16)
    chosen = experts_chosen[:, 0]
    gates = gate_scores[:, 0]
    flat_index, token_table, gate_table = slot_tables(chosen, gates)
    head_rows = jnp.arange(head_count, dtype=jnp.int32)[:, None]
    head_column = jnp.arange(head_count, dtype=jnp.int32)[:, None, None]
    input_slots = attended[token_table, head_column].reshape(
        group_count, local_experts, CAP, head_size
    )
    cot_rows = cotangent[0]
    grad_slots = (gate_table[..., None] * cot_rows[token_table].astype(jnp.float32)).astype(
        jnp.bfloat16
    )
    grad_slots = grad_slots.reshape(group_count, local_experts, CAP, model_width)
    slot_rows = lax.all_to_all(input_slots, "exp", split_axis=0, concat_axis=0, tiled=True)
    outputs = lax.all_to_all(
        jnp.einsum(
            "sxcd,xdf->sxcf", slot_rows, out_weight, preferred_element_type=jnp.float32
        ).astype(jnp.bfloat16),
        "exp",
        split_axis=0,
        concat_axis=0,
        tiled=True,
    )
    grad_piece = lax.all_to_all(grad_slots, "exp", split_axis=0, concat_axis=0, tiled=True)
    grad_back = lax.all_to_all(
        jnp.einsum("sxcf,xdf->sxcd", grad_piece, out_weight, preferred_element_type=jnp.float32),
        "exp",
        split_axis=0,
        concat_axis=0,
        tiled=True,
    )
    partial_value = jnp.einsum(
        "sxcd,sxcf->xdf", slot_rows, grad_piece, preferred_element_type=jnp.float32
    )
    out_weight_grad = lax.psum_scatter(partial_value, "ctx", scatter_dimension=2, tiled=True)
    out_flat = outputs.reshape(head_count, EXPERTS * CAP, model_width)
    picked = out_flat[head_rows, flat_index]
    weighted = picked.astype(jnp.float32) * gates.reshape(head_count, tok_rows * 2)[..., None]
    block_out = jnp.sum(weighted.reshape(head_count, tok_rows, 2, model_width), axis=(0, 2))
    back_flat = grad_back.reshape(head_count, EXPERTS * CAP, head_size)
    picked_back = back_flat[head_rows, flat_index]
    attended_grad = jnp.sum(picked_back.reshape(head_count, tok_rows, 2, head_size), axis=2)
    attended_grad = attended_grad.transpose(1, 0, 2).reshape(tok_rows, head_count * head_size)
    return (block_out[None], out_weight_grad, attended_grad[None])


def solution(mesh):
    return jax.shard_map(
        per_device,
        mesh=mesh,
        in_specs=(
            P("exp", "ctx", None),
            P("exp", "ctx", None),
            P("exp", "ctx", None),
            P(None, "exp", "ctx", None),
            P(None, "exp", "ctx", None),
            P("exp", None, None),
            P("exp", "ctx", None),
        ),
        out_specs=(P("exp", "ctx", None), P("exp", None, "ctx"), P("exp", "ctx", None)),
        check_vma=False,
    )
```

profile of v0, /device:TPU:25, one launch (start us, length us, event | category | flops | bytes accessed | tf_op | source)
XLA Modules:
  0.0 456.1 jit_solution(14560301036366980418)
XLA Ops:
  7.2 0.0 copy-start
  7.2 0.9 copy.90
  8.1 0.1 eq.47
  8.2 0.1 eq.51
  8.4 1.2 reduce-window.6
  9.5 0.2 slice_reduce_fusion
  9.8 0.1 fusion.34
  9.9 0.4 fusion.27
  10.3 0.1 reshape.197
  10.4 0.8 copy.96
  11.2 0.1 mul.93
  11.4 0.2 fusion.29
  11.5 0.0 copy-done
  11.5 5.4 %gather_fusion.2 = bf16[640,4096]{1,0:T(8,128)(2,1)} fusion(bf16[128,4096]{1,0:T(8,128)(2,1)S(1)} %bitcast.103, s32[1024]{0:T(1024)S(1)} %pad_clamp_fusion), kind=kCustom, calls=%fused_computation.2 | custom fusion | bytes 10488320 | tf_op jit(solution)/shard_map/gather | solution.py:83
  16.9 6.9 %fusion.12 = bf16[16,1,40,4096]{3,2,1,0:T(8,128)(2,1)} fusion(bf16[16,1,40,4096]{3,2,1,0:T(8,128)(2,1)} %bitcast.106, f32[16,40]{1,0:T(8,128)S(1)} %bitcast.113), kind=kLoop, calls=%fused_computation.21 | loop fusion | flops 7864320 | bytes 10488320 | tf_op jit(solution)/shard_map/convert_element_type | solution.py:83
  23.8 0.0 copy-start.3
  23.8 8.6 %all-to-all-start.2 = ((bf16[16,1,40,4096]{3,2,1,0:T(8,128)(2,1)}), bf16[16,1,40,4096]{3,2,1,0:T(8,128)(2,1)}, u32[]{:S(2)}, u32[]{:S(2)}) async-start(bf16[16,1,40,4096]{3,2,1,0:T(8,128)(2,1)} %fusion.12), calls=%async_computation.2 | async-start | bytes 10485760 | tf_op jit(solution)/shard_map/all_to_all | solution.py:97
  32.4 0.0 all-gather.3.cloned.1.call-start
  32.4 0.7 all-gather.3.cloned.1.call-update
  33.1 0.0 all-gather.5.cloned.1.call-start
  33.1 0.7 all-gather.5.cloned.1.call-update
  33.9 0.1 reshape.183
  33.9 99.5 %all-gather.3.cloned.1.call-done = bf16[1,4096,256]{2,1,0:T(8,128)(2,1)} async-done(((bf16[1,128,256]{2,1,0:T(8,128)(2,1)}), bf16[1,4096,256]{2,1,0:T(8,128)(2,1)}) %all-gather.3.cloned.1.call-update) | async-done | bytes 2097168 | tf_op jit(solution)/shard_map/all_gather | solution.py:44
  133.5 71.7 %all-gather.5.cloned.1.call-done = bf16[1,4096,256]{2,1,0:T(8,128)(2,1)} async-done(((bf16[1,128,256]{2,1,0:T(8,128)(2,1)}), bf16[1,4096,256]{2,1,0:T(8,128)(2,1)}) %all-gather.5.cloned.1.call-update) | async-done | bytes 2097168 | tf_op jit(solution)/shard_map/all_gather | solution.py:45
  205.2 0.0 copy-done.3
  205.2 0.0 copy-start.2
  205.2 18.6 %conditional.1 = (f32[2,128]{1,0:T(2,128)S(1)}, f32[2,128,128]{2,1,0:T(8,128)S(1)}) conditional(s32[]{:T(128)} %convert_element_type.74, (s32[]{:T(128)}, s32[128]{0:T(128)S(1)}, bf16[1,128,256]{2,1,0:T(8,128)(2,1)S(1)}, bf16[1,4096,256]{2,1,0:T(8,128)(2,1)}, bf16[1,4096,256]{2,1,0:T(8,128)(2,1)}) %tuple.33, () %tuple.17), branch_computations={%region_0.3_spmd, %region_3.4_spmd} | conditional | flops 546832256 | bytes 44375600 | solution.py:70
  205.2 0.4 iota_compare_fusion
  205.6 4.0 squeeze.6
  209.6 2.9 fusion.41
  212.5 0.0 copy-start.1
  212.5 2.1 copy-done.1
  214.6 1.1 fusion.2
  215.7 4.0 squeeze.7
  219.6 4.2 fusion.3
  223.9 0.1 fusion.33
  224.0 0.1 copy.92
  224.0 5.5 %gather_fusion = bf16[640,128]{1,0:T(8,128)(2,1)} fusion(bf16[128,2,128]{2,1,0:T(2,128)(2,1)S(1)} %copy.92, s32[640]{0:T(1024)S(1)} %reshape.183), kind=kCustom, calls=%fused_computation | custom fusion | bytes 332800 | tf_op jit(solution)/shard_map/gather | solution.py:79
  229.6 0.0 all-to-all-done.2
  229.6 8.9 %all-to-all-start = ((bf16[16,1,40,128]{3,2,1,0:T(8,128)(2,1)}), bf16[16,1,40,128]{3,2,1,0:T(8,128)(2,1)S(1)}, u32[]{:S(2)}, u32[]{:S(2)}) async-start(bf16[16,1,40,128]{3,2,1,0:T(8,128)(2,1)} %bitcast.5), calls=%async_computation | async-start | bytes 327680 | tf_op jit(solution)/shard_map/all_to_all | solution.py:87
  238.5 0.0 copy-done.2
  238.5 4.7 %fusion.22 = f32[16,1,40,128]{3,2,1,0:T(8,128)} fusion(bf16[16,1,40,4096]{3,2,1,0:T(8,128)(2,1)} %all-to-all-done.2, bf16[1,128,4096]{2,1,0:T(8,128)(2,1)S(1)} %copy-done.2), kind=kOutput, calls=%fused_computation.31 | convolution fusion | flops 671088640 | bytes 6619136 | tf_op jit(solution)/shard_map/sxcf,xdf->sxcd/dot_general | solution.py:99
  243.2 4.3 all-to-all-done
  247.5 5.2 %all-to-all-start.3 = ((f32[16,1,40,128]{3,2,1,0:T(8,128)}), f32[16,1,40,128]{3,2,1,0:T(8,128)S(1)}, u32[]{:S(2)}, u32[]{:S(2)}) async-start(f32[16,1,40,128]{3,2,1,0:T(8,128)} %fusion.22), calls=%async_computation.4 | async-start | bytes 655360 | tf_op jit(solution)/shard_map/all_to_all | solution.py:98
  252.7 3.9 fusion.14
  256.6 7.5 %all-to-all-done.3 = f32[16,1,40,128]{3,2,1,0:T(8,128)S(1)} async-done(((f32[16,1,40,128]{3,2,1,0:T(8,128)}), f32[16,1,40,128]{3,2,1,0:T(8,128)S(1)}, u32[]{:S(2)}, u32[]{:S(2)}) %all-to-all-start.3) | async-done | bytes 327712 | tf_op jit(solution)/shard_map/all_to_all | solution.py:98
  264.1 6.8 %all-to-all-start.1 = ((bf16[16,1,40,4096]{3,2,1,0:T(8,128)(2,1)}), bf16[16,1,40,4096]{3,2,1,0:T(8,128)(2,1)}, u32[]{:S(2)}, u32[]{:S(2)}) async-start(bf16[16,1,40,4096]{3,2,1,0:T(8,128)(2,1)} %fusion.14), calls=%async_computation.1 | async-start | bytes 10485760 | tf_op jit(solution)/shard_map/all_to_all | solution.py:88
  270.9 0.0 copy-start.4
  270.9 0.0 reduce-scatter.2.cloned.1.call-start
  271.0 4.8 %fusion.19 = f32[1,128,4096]{2,1,0:T(8,128)} fusion(bf16[16,1,40,4096]{3,2,1,0:T(8,128)(2,1)} %all-to-all-done.2, bf16[16,1,40,128]{3,2,1,0:T(8,128)(2,1)S(1)} %all-to-all-done), kind=kOutput, calls=%fused_computation.30 | convolution fusion | flops 671088640 | bytes 7503872 | tf_op jit(solution)/shard_map/sxcd,sxcf->xdf/dot_general | solution.py:105
  275.8 0.0 reduce-scatter.2.cloned.1.call-update
  275.8 0.0 copy-done.4
  275.8 0.1 copy.95
  276.0 0.1 mul.92
  276.1 3.7 gather_fusion.3
  279.8 0.3 reduce_sum.73
  280.1 0.1 copy.100
  280.2 0.8 copy.101
  281.0 130.3 %all-to-all-done.1 = bf16[16,1,40,4096]{3,2,1,0:T(8,128)(2,1)} async-done(((bf16[16,1,40,4096]{3,2,1,0:T(8,128)(2,1)}), bf16[16,1,40,4096]{3,2,1,0:T(8,128)(2,1)}, u32[]{:S(2)}, u32[]{:S(2)}) %all-to-all-start.1) | async-done | bytes 5242912 | tf_op jit(solution)/shard_map/all_to_all | solution.py:88
  411.3 17.7 %gather_fusion.1 = bf16[512,4096]{1,0:T(8,128)(2,1)} fusion(bf16[2,320,4096]{2,1,0:T(8,128)(2,1)} %bitcast.13, s32[512]{0:T(512)S(1)} %bitcast.105), kind=kCustom, calls=%fused_computation.1 | custom fusion | bytes 8392704 | tf_op jit(solution)/shard_map/gather | solution.py:110
  429.0 6.0 %fusion.13 = f32[256,4096]{1,0:T(8,128)} fusion(bf16[2,256,4096]{2,1,0:T(8,128)(2,1)} %bitcast.108, f32[2,256]{1,0:T(2,128)S(1)} %mul.93), kind=kLoop, calls=%fused_computation.23 | loop fusion | flops 5242880 | bytes 8390656 | tf_op jit(solution)/shard_map/reduce_sum | solution.py:112
  434.9 5.8 %reduce_sum.70 = f32[128,2,4096]{2,1,0:T(2,128)} reshape(f32[256,4096]{1,0:T(8,128)} %fusion.13) | data formatting | bytes 8388608 | tf_op jit(solution)/shard_map/reduce_sum | solution.py:112
  440.8 8.8 %reduce_sum.71 = f32[128,4096]{1,0:T(8,128)} reduce(f32[128,2,4096]{2,1,0:T(2,128)} %reduce_sum.70, f32[]{:T(128)} %constant.61.clone.1), dimensions={1}, to_apply=%region_9.10 | reduce | flops 524288 | bytes 6291460 | tf_op jit(solution)/shard_map/reduce_sum | solution.py:112
  449.6 0.0 reduce-scatter.2.cloned.1.call-done
  (15 shorter events, 0.1 us)
Async XLA Ops:
  7.2 4.4 copy-start
  23.8 181.4 %copy-start.3 = (bf16[1,128,256]{2,1,0:T(8,128)(2,1)S(1)}, bf16[1,128,256]{2,1,0:T(8,128)(2,1)}, u32[]{:S(2)}) copy-start(bf16[1,128,256]{2,1,0:T(8,128)(2,1)} %param.9) | copy-start | bytes 196612
  23.8 205.8 %all-to-all-start.2 = ((bf16[16,1,40,4096]{3,2,1,0:T(8,128)(2,1)}), bf16[16,1,40,4096]{3,2,1,0:T(8,128)(2,1)}, u32[]{:S(2)}, u32[]{:S(2)}) async-start(bf16[16,1,40,4096]{3,2,1,0:T(8,128)(2,1)} %fusion.12), calls=%async_computation.2 | async-start | bytes 10485760 | tf_op jit(solution)/shard_map/all_to_all | solution.py:97
  32.4 101.1 %all-gather.3.cloned.1.call-start = ((), (), s32[]{:S(2)}) async-start(), calls=%async_computation.5 | async-start | bytes 2162688 | tf_op jit(solution)/shard_map/all_gather | solution.py:44
  33.1 172.1 %all-gather.5.cloned.1.call-start = ((), (), s32[]{:S(2)}) async-start(), calls=%async_computation.6 | async-start | bytes 2162688 | tf_op jit(solution)/shard_map/all_gather | solution.py:45
  205.2 33.3 %copy-start.2 = (bf16[1,128,4096]{2,1,0:T(8,128)(2,1)S(1)}, bf16[1,128,4096]{2,1,0:T(8,128)(2,1)}, u32[]{:S(2)}) copy-start(bf16[1,128,4096]{2,1,0:T(8,128)(2,1)} %param.14) | copy-start | bytes 3145732
  212.5 2.1 copy-start.1
  229.6 18.0 %all-to-all-start = ((bf16[16,1,40,128]{3,2,1,0:T(8,128)(2,1)}), bf16[16,1,40,128]{3,2,1,0:T(8,128)(2,1)S(1)}, u32[]{:S(2)}, u32[]{:S(2)}) async-start(bf16[16,1,40,128]{3,2,1,0:T(8,128)(2,1)} %bitcast.5), calls=%async_computation | async-start | bytes 327680 | tf_op jit(solution)/shard_map/all_to_all | solution.py:87
  247.5 16.6 %all-to-all-start.3 = ((f32[16,1,40,128]{3,2,1,0:T(8,128)}), f32[16,1,40,128]{3,2,1,0:T(8,128)S(1)}, u32[]{:S(2)}, u32[]{:S(2)}) async-start(f32[16,1,40,128]{3,2,1,0:T(8,128)} %fusion.22), calls=%async_computation.4 | async-start | bytes 655360 | tf_op jit(solution)/shard_map/all_to_all | solution.py:98
  264.1 147.2 %all-to-all-start.1 = ((bf16[16,1,40,4096]{3,2,1,0:T(8,128)(2,1)}), bf16[16,1,40,4096]{3,2,1,0:T(8,128)(2,1)}, u32[]{:S(2)}, u32[]{:S(2)}) async-start(bf16[16,1,40,4096]{3,2,1,0:T(8,128)(2,1)} %fusion.14), calls=%async_computation.1 | async-start | bytes 10485760 | tf_op jit(solution)/shard_map/all_to_all | solution.py:88
  270.9 4.9 %copy-start.4 = (s32[2,1,128,2]{2,3,1,0:T(2,128)S(1)}, s32[2,1,128,2]{2,3,1,0:T(2,128)}, u32[]{:S(2)}) copy-start(s32[2,1,128,2]{2,3,1,0:T(2,128)} %param.12) | copy-start | bytes 6148
  270.9 178.7 %reduce-scatter.2.cloned.1.call-start = ((), (), s32[]{:S(2)}) async-start(), calls=%async_computation.7 | async-start | bytes 2162688 | tf_op jit(solution)/shard_map/reduce_scatter | solution.py:108
Sparse Core Ops, SparseCore 0:
  35.3 98.0 all-gather.2
  135.6 69.5 all-gather.4
  275.9 156.3 reduce-scatter.1
where the time goes:
time: 457 us; the launch traced here: 456 us
  waiting for transfers between devices  315 us (69%)
  local copies, waits for them, and re-layouts  51.8 us (11%)
  starting transfers between devices  29.5 us (6%)
  other arithmetic  25.4 us (6%)
  matrix products  20.6 us (5%)
  between operations  14 us (3%)
    all_to_all x1, waiting for transfers between devices, per_device(): lax.all_to_all(jnp.einsum('sxcd,xdf->sxcf', slot_rows, out_weight, prefer...  130 us
    all_gather x1, waiting for transfers between devices, per_device(): key_piece = lax.all_gather(keys, 'ctx', axis=1, tiled=True)  99.5 us
    all_gather x1, waiting for transfers between devices, per_device(): value_piece = lax.all_gather(values, 'ctx', axis=1, tiled=True)  71.7 us
    gather x1, local copies, waits for them, and re-layouts, per_device(): picked = out_flat[head_rows, flat_index]  17.7 us
    reduce_sum x2, other arithmetic, per_device(): jnp.sum(weighted.reshape(head_count, tok_rows, 2, model_width), axis=(0, 2))  14.8 us
  transfers between devices with their start and end apart: 7, of which 5 were waited for; matrix products, arithmetic and copies ran while one was open for 17% of the time, Pallas kernels for 0%

commit v1 on v0

--- a/solution.py
+++ b/solution.py
@@ -41,8 +41,11 @@
         jnp.zeros((head_count, tok_rows), jnp.float32),
         jnp.zeros((head_count, tok_rows, head_size), jnp.float32),
     )
-    key_piece = lax.all_gather(keys, "ctx", axis=1, tiled=True)
-    value_piece = lax.all_gather(values, "ctx", axis=1, tiled=True)
+    key_piece, value_piece = jnp.split(
+        lax.all_gather(jnp.concatenate([keys, values], axis=0), "ctx", axis=1, tiled=True),
+        [keys.shape[0]],
+        axis=0,
+    )
     key_count = key_piece.shape[1]
 
     def compute(state_now):

time: 457 us -> 391 us (0.86)
  the two profiles are of different devices: /device:TPU:25 before, /device:TPU:22 now
where the time goes in v1:
time: 391 us; the launch traced here: 390 us
  waiting for transfers between devices  248 us (63%)
  local copies, waits for them, and re-layouts  46.3 us (12%)
  starting transfers between devices  38.9 us (10%)
  other arithmetic  26 us (7%)
  matrix products  15.9 us (4%)
  between operations  14.3 us (4%)
    all_gather x1, waiting for transfers between devices, per_device(): lax.all_gather(jnp.concatenate([keys, values], axis=0), 'ctx', axis=1, ti...  119 us
    all_to_all x1, waiting for transfers between devices, per_device(): lax.all_to_all(jnp.einsum('sxcd,xdf->sxcf', slot_rows, out_weight, prefer...  108 us
    gather x1, local copies, waits for them, and re-layouts, per_device(): picked = out_flat[head_rows, flat_index]  17.5 us
    reduce_sum x2, other arithmetic, per_device(): jnp.sum(weighted.reshape(head_count, tok_rows, 2, model_width), axis=(0, 2))  14.8 us
    reduce_scatter x1, waiting for transfers between devices, per_device(): lax.psum_scatter(partial_value, 'ctx', scatter_dimension=2, tiled=True)  11.9 us
    all_to_all x1, starting transfers between devices, per_device(): lax.all_to_all(input_slots, 'exp', split_axis=0, concat_axis=0, tiled=True)  11.6 us
    all_to_all x1, starting transfers between devices, per_device(): lax.all_to_all(grad_slots, 'exp', split_axis=0, concat_axis=0, tiled=True)  10.1 us
    all_to_all x1, starting transfers between devices, per_device(): lax.all_to_all(jnp.einsum('sxcd,xdf->sxcf', slot_rows, out_weight, prefer...  8.94 us
  transfers between devices with their start and end apart: 6, of which 6 were waited for; matrix products, arithmetic and copies ran while one was open for 18% of the time, Pallas kernels for 0%

profile of v1, /device:TPU:22, one launch (start us, length us, event | category | flops | bytes accessed | tf_op | source)
XLA Modules:
  0.0 389.8 jit_solution(9114559489754478823)
XLA Ops:
  7.2 0.0 copy-start
  7.2 0.9 copy.100
  8.1 0.1 eq.51
  8.2 0.1 eq.47
  8.4 1.2 reduce-window.6
  9.5 0.2 slice_reduce_fusion
  9.8 0.1 fusion.32
  9.9 0.4 fusion.25
  10.3 0.8 copy.106
  11.1 0.1 mul.93
  11.3 0.1 reshape.197
  11.4 0.2 fusion.27
  11.5 0.0 copy-done
  11.5 5.4 %gather_fusion.2 = bf16[640,4096]{1,0:T(8,128)(2,1)} fusion(bf16[128,4096]{1,0:T(8,128)(2,1)S(1)} %bitcast.107, s32[1024]{0:T(1024)S(1)} %pad_clamp_fusion), kind=kCustom, calls=%fused_computation.2 | custom fusion | bytes 10488320 | tf_op jit(solution)/shard_map/gather | solution.py:86
  16.9 6.9 %fusion.10 = bf16[16,1,40,4096]{3,2,1,0:T(8,128)(2,1)} fusion(bf16[16,1,40,4096]{3,2,1,0:T(8,128)(2,1)} %bitcast.110, f32[16,40]{1,0:T(8,128)S(1)} %bitcast.119), kind=kLoop, calls=%fused_computation.19 | loop fusion | flops 7864320 | bytes 10488320 | tf_op jit(solution)/shard_map/convert_element_type | solution.py:86
  23.8 0.0 copy-start.4
  23.8 0.0 copy-start.5
  23.8 10.1 %all-to-all-start.2 = ((bf16[16,1,40,4096]{3,2,1,0:T(8,128)(2,1)}), bf16[16,1,40,4096]{3,2,1,0:T(8,128)(2,1)}, u32[]{:S(2)}, u32[]{:S(2)}) async-start(bf16[16,1,40,4096]{3,2,1,0:T(8,128)(2,1)} %fusion.10), calls=%async_computation.2 | async-start | bytes 10485760 | tf_op jit(solution)/shard_map/all_to_all | solution.py:100
  33.9 0.0 all-gather.2.cloned.1.call-start
  33.9 0.0 copy-done.3
  34.0 0.1 copy.99
  34.1 0.0 copy-done.4
  34.1 0.1 copy.98
  34.2 0.7 pad_maximum_fusion
  34.9 0.0 all-gather.2.cloned.1.call-update
  34.9 0.1 reshape.183
  35.0 119.2 %all-gather.2.cloned.1.call-done = bf16[2,4096,256]{1,2,0:T(8,128)(2,1)} async-done(((bf16[2,128,256]{1,2,0:T(8,128)(2,1)}), bf16[2,4096,256]{1,2,0:T(8,128)(2,1)}) %all-gather.2.cloned.1.call-update) | async-done | bytes 4194320 | tf_op jit(solution)/shard_map/all_gather | solution.py:45
  154.2 0.0 copy-done.5
  154.2 8.1 %conditional.1 = (f32[2,128]{1,0:T(2,128)S(1)}, f32[2,128,128]{2,1,0:T(8,128)S(1)}) conditional(s32[]{:T(128)} %convert_element_type.74, (s32[]{:T(128)}, s32[128]{0:T(128)S(1)}, bf16[1,128,256]{2,1,0:T(8,128)(2,1)S(1)}, bf16[2,4096,256]{1,2,0:T(8,128)(2,1)}) %tuple.32, () %tuple.17), branch_computations={%region_0.3_spmd, %region_3.4_spmd} | conditional | flops 546832256 | bytes 35986992 | solution.py:73
  154.2 3.9 %fusion.39 = (bf16[1,4096,256]{1,2,0:T(8,128)(2,1)}, bf16[1,4096,256]{1,2,0:T(8,128)(2,1)S(1)}) fusion(bf16[2,4096,256]{1,2,0:T(8,128)(2,1)} %get-tuple-element.17), kind=kLoop, calls=%fused_computation.65 | loop fusion | bytes 8388608 | tf_op jit(solution)/shard_map/split | solution.py:44
  158.2 0.4 iota_compare_fusion
  158.6 1.3 fusion.40
  159.8 0.0 copy-start.1
  159.9 1.1 fusion.2
  160.9 0.5 copy-done.1
  161.4 0.9 fusion.3
  162.4 0.1 fusion.31
  162.5 0.1 copy.102
  162.6 5.5 %gather_fusion = bf16[640,128]{1,0:T(8,128)(2,1)} fusion(bf16[128,2,128]{2,1,0:T(2,128)(2,1)S(1)} %copy.102, s32[640]{0:T(1024)S(1)} %reshape.183), kind=kCustom, calls=%fused_computation | custom fusion | bytes 332800 | tf_op jit(solution)/shard_map/gather | solution.py:82
  168.1 2.6 all-to-all-done.2
  170.7 11.6 %all-to-all-start = ((bf16[16,1,40,128]{3,2,1,0:T(8,128)(2,1)}), bf16[16,1,40,128]{3,2,1,0:T(8,128)(2,1)S(1)}, u32[]{:S(2)}, u32[]{:S(2)}) async-start(bf16[16,1,40,128]{3,2,1,0:T(8,128)(2,1)} %bitcast.7), calls=%async_computation | async-start | bytes 327680 | tf_op jit(solution)/shard_map/all_to_all | solution.py:90
  182.3 5.0 %fusion.20 = f32[16,1,40,128]{3,2,1,0:T(8,128)} fusion(bf16[16,1,40,4096]{3,2,1,0:T(8,128)(2,1)} %all-to-all-done.2, bf16[1,128,4096]{2,1,0:T(8,128)(2,1)} %param.14), kind=kOutput, calls=%fused_computation.29 | convolution fusion | flops 671088640 | bytes 6619136 | tf_op jit(solution)/shard_map/sxcf,xdf->sxcd/dot_general | solution.py:102
  187.4 1.5 all-to-all-done
  188.9 8.2 %all-to-all-start.3 = ((f32[16,1,40,128]{3,2,1,0:T(8,128)}), f32[16,1,40,128]{3,2,1,0:T(8,128)S(1)}, u32[]{:S(2)}, u32[]{:S(2)}) async-start(f32[16,1,40,128]{3,2,1,0:T(8,128)} %fusion.20), calls=%async_computation.4 | async-start | bytes 655360 | tf_op jit(solution)/shard_map/all_to_all | solution.py:101
  197.0 0.0 copy-done.2
  197.0 3.9 fusion.12
  200.9 5.0 %all-to-all-done.3 = f32[16,1,40,128]{3,2,1,0:T(8,128)S(1)} async-done(((f32[16,1,40,128]{3,2,1,0:T(8,128)}), f32[16,1,40,128]{3,2,1,0:T(8,128)S(1)}, u32[]{:S(2)}, u32[]{:S(2)}) %all-to-all-start.3) | async-done | bytes 327712 | tf_op jit(solution)/shard_map/all_to_all | solution.py:101
  205.9 8.9 %all-to-all-start.1 = ((bf16[16,1,40,4096]{3,2,1,0:T(8,128)(2,1)}), bf16[16,1,40,4096]{3,2,1,0:T(8,128)(2,1)}, u32[]{:S(2)}, u32[]{:S(2)}) async-start(bf16[16,1,40,4096]{3,2,1,0:T(8,128)(2,1)} %fusion.12), calls=%async_computation.1 | async-start | bytes 10485760 | tf_op jit(solution)/shard_map/all_to_all | solution.py:91
  214.9 0.0 reduce-scatter.2.cloned.1.call-start
  214.9 4.8 %fusion.17 = f32[1,128,4096]{2,1,0:T(8,128)} fusion(bf16[16,1,40,4096]{3,2,1,0:T(8,128)(2,1)} %all-to-all-done.2, bf16[16,1,40,128]{3,2,1,0:T(8,128)(2,1)S(1)} %all-to-all-done), kind=kOutput, calls=%fused_computation.28 | convolution fusion | flops 671088640 | bytes 7503872 | tf_op jit(solution)/shard_map/sxcd,sxcf->xdf/dot_general | solution.py:108
  219.7 0.0 reduce-scatter.2.cloned.1.call-update
  219.8 0.0 copy-done.6
  219.8 0.1 copy.105
  219.9 0.1 mul.92
  220.1 3.7 gather_fusion.3
  223.8 0.3 reduce_sum.73
  224.1 0.1 copy.110
  224.2 0.8 copy.111
  224.9 108.0 %all-to-all-done.1 = bf16[16,1,40,4096]{3,2,1,0:T(8,128)(2,1)} async-done(((bf16[16,1,40,4096]{3,2,1,0:T(8,128)(2,1)}), bf16[16,1,40,4096]{3,2,1,0:T(8,128)(2,1)}, u32[]{:S(2)}, u32[]{:S(2)}) %all-to-all-start.1) | async-done | bytes 5242912 | tf_op jit(solution)/shard_map/all_to_all | solution.py:91
  332.9 17.5 %gather_fusion.1 = bf16[512,4096]{1,0:T(8,128)(2,1)} fusion(bf16[2,320,4096]{2,1,0:T(8,128)(2,1)} %bitcast.15, s32[512]{0:T(512)S(1)} %bitcast.109), kind=kCustom, calls=%fused_computation.1 | custom fusion | bytes 8392704 | tf_op jit(solution)/shard_map/gather | solution.py:113
  350.4 6.0 %fusion.11 = f32[256,4096]{1,0:T(8,128)} fusion(bf16[2,256,4096]{2,1,0:T(8,128)(2,1)} %bitcast.112, f32[2,256]{1,0:T(2,128)S(1)} %mul.93), kind=kLoop, calls=%fused_computation.21 | loop fusion | flops 5242880 | bytes 8390656 | tf_op jit(solution)/shard_map/reduce_sum | solution.py:115
  356.4 5.8 %reduce_sum.70 = f32[128,2,4096]{2,1,0:T(2,128)} reshape(f32[256,4096]{1,0:T(8,128)} %fusion.11) | data formatting | bytes 8388608 | tf_op jit(solution)/shard_map/reduce_sum | solution.py:115
  362.2 8.8 %reduce_sum.71 = f32[128,4096]{1,0:T(8,128)} reduce(f32[128,2,4096]{2,1,0:T(2,128)} %reduce_sum.70, f32[]{:T(128)} %constant.61.clone.1), dimensions={1}, to_apply=%region_9.10 | reduce | flops 524288 | bytes 6291460 | tf_op jit(solution)/shard_map/reduce_sum | solution.py:115
  371.0 11.9 %reduce-scatter.2.cloned.1.call-done = f32[1,128,128]{2,1,0:T(8,128)} async-done(((f32[1,128,4096]{2,1,0:T(8,128)}), f32[1,128,128]{2,1,0:T(8,128)}) %reduce-scatter.2.cloned.1.call-update) | async-done | bytes 65552 | tf_op jit(solution)/shard_map/reduce_scatter | solution.py:111
  (18 shorter events, 0.1 us)
Async XLA Ops:
  7.2 4.4 %copy-start = (bf16[1,128,4096]{2,1,0:T(8,128)(2,1)S(1)}, bf16[1,128,4096]{2,1,0:T(8,128)(2,1)}, u32[]{:S(2)}) copy-start(bf16[1,128,4096]{2,1,0:T(8,128)(2,1)} %param.15) | copy-start | bytes 3145732
  23.8 10.2 %copy-start.3 = (bf16[1,128,256]{2,1,0:T(8,128)(2,1)S(1)}, bf16[1,128,256]{2,1,0:T(8,128)(2,1)}, u32[]{:S(2)}) copy-start(bf16[1,128,256]{2,1,0:T(8,128)(2,1)} %param.11) | copy-start | bytes 196612
  23.8 10.3 %copy-start.4 = (bf16[1,128,256]{2,1,0:T(8,128)(2,1)S(1)}, bf16[1,128,256]{2,1,0:T(8,128)(2,1)}, u32[]{:S(2)}) copy-start(bf16[1,128,256]{2,1,0:T(8,128)(2,1)} %param.10) | copy-start | bytes 196612
  23.8 130.5 %copy-start.5 = (bf16[1,128,256]{2,1,0:T(8,128)(2,1)S(1)}, bf16[1,128,256]{2,1,0:T(8,128)(2,1)}, u32[]{:S(2)}) copy-start(bf16[1,128,256]{2,1,0:T(8,128)(2,1)} %param.9) | copy-start | bytes 196612
  23.8 146.9 %all-to-all-start.2 = ((bf16[16,1,40,4096]{3,2,1,0:T(8,128)(2,1)}), bf16[16,1,40,4096]{3,2,1,0:T(8,128)(2,1)}, u32[]{:S(2)}, u32[]{:S(2)}) async-start(bf16[16,1,40,4096]{3,2,1,0:T(8,128)(2,1)} %fusion.10), calls=%async_computation.2 | async-start | bytes 10485760 | tf_op jit(solution)/shard_map/all_to_all | solution.py:100
  33.9 120.3 %all-gather.2.cloned.1.call-start = ((), (), s32[]{:S(2)}) async-start(), calls=%async_computation.5 | async-start | bytes 4325376 | tf_op jit(solution)/shard_map/all_gather | solution.py:45
  159.8 1.6 copy-start.1
  168.1 28.9 %copy-start.2 = (bf16[1,128,4096]{2,1,0:T(8,128)(2,1)S(1)}, bf16[1,128,4096]{2,1,0:T(8,128)(2,1)}, u32[]{:S(2)}) copy-start(bf16[1,128,4096]{2,1,0:T(8,128)(2,1)} %param.14) | copy-start | bytes 3145732
  170.7 18.1 %all-to-all-start = ((bf16[16,1,40,128]{3,2,1,0:T(8,128)(2,1)}), bf16[16,1,40,128]{3,2,1,0:T(8,128)(2,1)S(1)}, u32[]{:S(2)}, u32[]{:S(2)}) async-start(bf16[16,1,40,128]{3,2,1,0:T(8,128)(2,1)} %bitcast.7), calls=%async_computation | async-start | bytes 327680 | tf_op jit(solution)/shard_map/all_to_all | solution.py:90
  188.9 17.1 %all-to-all-start.3 = ((f32[16,1,40,128]{3,2,1,0:T(8,128)}), f32[16,1,40,128]{3,2,1,0:T(8,128)S(1)}, u32[]{:S(2)}, u32[]{:S(2)}) async-start(f32[16,1,40,128]{3,2,1,0:T(8,128)} %fusion.20), calls=%async_computation.4 | async-start | bytes 655360 | tf_op jit(solution)/shard_map/all_to_all | solution.py:101
  205.9 127.0 %all-to-all-start.1 = ((bf16[16,1,40,4096]{3,2,1,0:T(8,128)(2,1)}), bf16[16,1,40,4096]{3,2,1,0:T(8,128)(2,1)}, u32[]{:S(2)}, u32[]{:S(2)}) async-start(bf16[16,1,40,4096]{3,2,1,0:T(8,128)(2,1)} %fusion.12), calls=%async_computation.1 | async-start | bytes 10485760 | tf_op jit(solution)/shard_map/all_to_all | solution.py:91
  214.9 4.9 %copy-start.6 = (s32[2,1,128,2]{2,3,1,0:T(2,128)S(1)}, s32[2,1,128,2]{2,3,1,0:T(2,128)}, u32[]{:S(2)}) copy-start(s32[2,1,128,2]{2,3,1,0:T(2,128)} %param.12) | copy-start | bytes 6148
  214.9 168.1 %reduce-scatter.2.cloned.1.call-start = ((), (), s32[]{:S(2)}) async-start(), calls=%async_computation.6 | async-start | bytes 2162688 | tf_op jit(solution)/shard_map/reduce_scatter | solution.py:111
Sparse Core Ops, SparseCore 0:
  37.3 116.8 all-gather.1
  219.9 163.0 reduce-scatter.1
